TPU v7x, 256 devices: a whole 4x4x8 slice. The times are simulated.
256 devices in a mesh: gx: 32 (over z, x), gy: 8 (over y, core).
Axes of the slice: x: 4, y: 4, z: 8, core: 2. Of those that a mesh axis runs over, the one named last changes fastest.
Arguments:
- field: bfloat16 [20, 256, 128, 256], P(None, 'gx', 'gy'), may hold values from -6 to 6
- cotangent: bfloat16 [20, 256, 128, 256], P(None, 'gx', 'gy'), may hold values from -6 to 6
- spectral_weight: bfloat16 [2, 20, 20, 24, 2304], P(None, None, None, 'gy', 'gx'), may hold values from -6 to 6
- pointwise_weight: bfloat16 [20, 20], replicated, may hold values from -1.25 to 1.25
- bias: float32 [20], replicated, may hold values from -1 to 1
Outputs:
- output: bfloat16 [20, 256, 128, 256], P(None, 'gx', 'gy')
- grad_field: bfloat16 [20, 256, 128, 256], P(None, 'gx', 'gy')
- grad_spectral: float32 [2, 20, 20, 24, 2304], P(None, None, None, 'gy', 'gx')
- grad_pointwise: float32 [20, 20], replicated
- grad_bias: float32 [20], replicated
All inputs are finite; a program needn't handle non-finite values.
Results may differ from a plain program's by a relative error of at most 0.0013.
Values sent between devices are 32-bit elements; how exact they have to be, the bound alone decides.
A program may use at most 128 MiB of HBM per device.

v0:
```python
import math
import jax
import jax.numpy as jnp
from jax import lax
from jax.sharding import PartitionSpec as P

MX = 24
MY = 24
MZ = 24
PRECISE = lax.Precision.HIGHEST
TWO_PI = 2.0 * math.pi


def angles(frequencies, places, length):
    product = places[:, None] * frequencies[None, :] % length
    return product.astype(jnp.float32) * (TWO_PI / length)


def frequency(position, kept_modes, length):
    return jnp.where(position < kept_modes, position, position - 2 * kept_modes + length)


def forward_y(values, phases):
    cosine_table = jnp.cos(phases)
    sine_table = jnp.sin(phases)
    with_cos = jnp.einsum("brcxy,yj->brcxj", values, cosine_table, precision=PRECISE)
    with_sin = jnp.einsum("brcxy,yj->brcxj", values, sine_table, precision=PRECISE)
    real_part = with_cos[:, 0] + with_sin[:, 1]
    imag_part = with_cos[:, 1] - with_sin[:, 0]
    return jnp.stack([real_part, imag_part], axis=1)


def inverse_y(values, phases):
    cosine_table = jnp.cos(phases)
    sine_table = jnp.sin(phases)
    with_cos = jnp.einsum("brcxj,yj->brcxy", values, cosine_table, precision=PRECISE)
    with_sin = jnp.einsum("brcxj,yj->brcxy", values, sine_table, precision=PRECISE)
    real_part = with_cos[:, 0] - with_sin[:, 1]
    imag_part = with_sin[:, 0] + with_cos[:, 1]
    return jnp.stack([real_part, imag_part], axis=1)


def local(field, cotangent, spectral_weight, pointwise_weight, bias):
    channels, rows_x, rows_y, depth_cells = field.shape
    blocks_z = spectral_weight.shape[3]
    pair_rows = spectral_weight.shape[4]
    width_x = 2 * MX
    width_y = 2 * MY
    full_x = rows_x * lax.axis_size("gx")
    full_y = rows_y * lax.axis_size("gy")
    cell_count = float(full_x * full_y * depth_cells)
    place_x = lax.axis_index("gx")
    place_y = lax.axis_index("gy")
    own_x = place_x * rows_x + jnp.arange(rows_x, dtype=jnp.int32)
    freq_x = frequency(jnp.arange(width_x, dtype=jnp.int32), MX, full_x)
    freq_y = frequency(jnp.arange(width_y, dtype=jnp.int32), MY, full_y)
    phases_full_y = angles(freq_y, jnp.arange(full_y, dtype=jnp.int32), full_y)
    z_phases = angles(
        jnp.arange(MZ, dtype=jnp.int32), jnp.arange(depth_cells, dtype=jnp.int32), depth_cells
    )
    table_z = jnp.stack([jnp.cos(z_phases), -jnp.sin(z_phases)], axis=2).reshape(
        depth_cells, 2 * MZ
    )
    kz_own = place_y * blocks_z + jnp.arange(blocks_z, dtype=jnp.int32)
    weight_z = (jnp.where(kz_own == 0, 1.0, 2.0).astype(jnp.float32) / cell_count)[None, :, None]
    own_first = place_x * pair_rows
    flat_width = blocks_z * 2 * channels

    def kx_terms(values, places, first_pair, count):
        kx_count = min(count // width_y + 2, width_x)
        kx_first = jnp.minimum(first_pair // width_y, width_x - kx_count)
        kx_ids = kx_first + jnp.arange(kx_count, dtype=jnp.int32)
        phases = angles(frequency(kx_ids, MX, full_x), places, full_x)
        cosine_table = jnp.cos(phases)
        sine_table = jnp.sin(phases)
        real_part = jnp.einsum(
            "bcxj,xi->ijbc", values[:, 0], cosine_table, precision=PRECISE
        ) + jnp.einsum("bcxj,xi->ijbc", values[:, 1], sine_table, precision=PRECISE)
        imag_part = jnp.einsum(
            "bcxj,xi->ijbc", values[:, 1], cosine_table, precision=PRECISE
        ) - jnp.einsum("bcxj,xi->ijbc", values[:, 0], sine_table, precision=PRECISE)
        terms = jnp.stack([real_part, imag_part], axis=3).reshape(kx_count * width_y, flat_width)
        offset = first_pair - kx_first * width_y
        return lax.dynamic_slice_in_dim(terms, offset, count, 0)

    def analyze(values):
        flat = values.reshape(-1, depth_cells)
        spectra = jnp.einsum("zk,mz->km", table_z, flat, precision=PRECISE).reshape(
            2 * MZ, channels, rows_x, rows_y
        )
        columns = lax.all_to_all(spectra, "gy", split_axis=0, concat_axis=3, tiled=True)
        mode_data = forward_y(columns.reshape(blocks_z, 2, channels, rows_x, full_y), phases_full_y)
        portion = lax.all_gather(mode_data, "gx", axis=3, tiled=True)
        places = jnp.arange(portion.shape[3], dtype=jnp.int32)
        owned = kx_terms(portion, places, own_first, pair_rows)
        return jnp.transpose(owned.reshape(pair_rows, blocks_z, 2, channels), (2, 3, 1, 0))

    def synthesize(spectrum):
        portion = lax.all_gather(spectrum, "gx", axis=3, tiled=True)
        blocks = portion.reshape(2, channels, blocks_z, width_x, width_y)
        phases = angles(freq_x, own_x, full_x)
        cosine_table = jnp.cos(phases)
        sine_table = jnp.sin(phases)
        real_part = jnp.einsum(
            "cbij,xi->bcxj", blocks[0], cosine_table, precision=PRECISE
        ) - jnp.einsum("cbij,xi->bcxj", blocks[1], sine_table, precision=PRECISE)
        imag_part = jnp.einsum(
            "cbij,xi->bcxj", blocks[0], sine_table, precision=PRECISE
        ) + jnp.einsum("cbij,xi->bcxj", blocks[1], cosine_table, precision=PRECISE)
        mode_data = jnp.stack([real_part, imag_part], axis=1)
        fields = inverse_y(mode_data, phases_full_y)
        columns = lax.all_to_all(fields, "gy", split_axis=4, concat_axis=0, tiled=True)
        flat = columns.reshape(2 * MZ, -1)
        return jnp.einsum("km,zk->mz", flat, table_z, precision=PRECISE).reshape(
            channels, rows_x, rows_y, depth_cells
        )

    weights = spectral_weight.astype(jnp.float32)
    widened = field.astype(jnp.float32)
    spec_u = analyze(widened)
    mixed_re = jnp.einsum("cobp,cbp->obp", weights[0], spec_u[0], precision=PRECISE) - jnp.einsum(
        "cobp,cbp->obp", weights[1], spec_u[1], precision=PRECISE
    )
    mixed_im = jnp.einsum("cobp,cbp->obp", weights[0], spec_u[1], precision=PRECISE) + jnp.einsum(
        "cobp,cbp->obp", weights[1], spec_u[0], precision=PRECISE
    )
    mixed_modes = jnp.stack([mixed_re, mixed_im]) * weight_z
    conv = synthesize(mixed_modes)
    pointwise = jnp.dot(
        pointwise_weight.T, field.reshape(channels, -1), preferred_element_type=jnp.float32
    ).reshape(field.shape)
    preact = pointwise + bias[:, None, None, None] + conv
    activated, pullback = jax.vjp(jax.nn.gelu, preact)
    gradient = pullback(cotangent.astype(jnp.float32))[0]
    grad_mix = analyze(gradient) * weight_z
    spec_re = jnp.einsum("cobp,obp->cbp", weights[0], grad_mix[0], precision=PRECISE) + jnp.einsum(
        "cobp,obp->cbp", weights[1], grad_mix[1], precision=PRECISE
    )
    spec_im = jnp.einsum("cobp,obp->cbp", weights[0], grad_mix[1], precision=PRECISE) - jnp.einsum(
        "cobp,obp->cbp", weights[1], grad_mix[0], precision=PRECISE
    )
    grad_spec = jnp.stack([spec_re, spec_im])
    weight_re = jnp.einsum("cbp,obp->cobp", spec_u[0], grad_mix[0], precision=PRECISE) + jnp.einsum(
        "cbp,obp->cobp", spec_u[1], grad_mix[1], precision=PRECISE
    )
    weight_im = jnp.einsum("cbp,obp->cobp", spec_u[0], grad_mix[1], precision=PRECISE) - jnp.einsum(
        "cbp,obp->cobp", spec_u[1], grad_mix[0], precision=PRECISE
    )
    grad_spectral = jnp.stack([weight_re, weight_im])
    returned = synthesize(grad_spec)
    grad_flat = gradient.reshape(channels, -1)
    back_point = jnp.dot(
        pointwise_weight.astype(jnp.float32), grad_flat, precision=PRECISE
    ).reshape(field.shape)
    grad_field = (back_point + returned).astype(jnp.bfloat16)
    local_weight = jnp.dot(widened.reshape(channels, -1), grad_flat.T, precision=PRECISE)
    local_bias = jnp.sum(grad_flat, axis=1)
    summed_weight, summed_bias = lax.psum((local_weight, local_bias), ("gx", "gy"))
    shrink = cell_count ** (-0.5)
    return (
        activated.astype(jnp.bfloat16),
        grad_field,
        grad_spectral,
        summed_weight * shrink,
        summed_bias * shrink,
    )


def solution(mesh):
    placed = (
        P(None, "gx", "gy", None),
        P(None, "gx", "gy", None),
        P(None, None, None, "gy", "gx"),
        P(),
        P(),
    )
    return jax.shard_map(
        local,
        mesh=mesh,
        in_specs=placed,
        out_specs=(
            P(None, "gx", "gy", None),
            P(None, "gx", "gy", None),
            P(None, None, None, "gy", "gx"),
            P(),
            P(),
        ),
        check_vma=False,
    )
```

profile of v0, /device:TPU:1, one launch (start us, length us, event | category | flops | bytes accessed | tf_op | source)
XLA Modules:
  0.0 803.7 jit_solution(9280649417124723916)
XLA Ops:
  10.4 3.8 copy.294
  14.2 5.5 reshape.223
  19.7 6.6 all-to-all-start
  26.5 9.0 %all-to-all-done = f32[8,1,15360]{2,1,0:T(1,128)S(1)} async-done(((f32[8,1,15360]{2,1,0:T(1,128)}), f32[8,1,15360]{2,1,0:T(1,128)S(1)}, u32[]{:S(2)}, u32[]{:S(2)}) %all-to-all-start) | async-done | bytes 491552 | tf_op jit(solution)/shard_map/all_to_all | solution.py:91
  37.9 5.3 reshape.224
  43.3 6.3 copy.295
  49.6 3.1 reshape.183
  56.2 141.7 %all-gather.5.cloned.1.call-done = f32[3,2,20,256,48]{4,3,2,1,0:T(8,128)} async-done(((f32[3,2,20,8,48]{4,3,2,1,0:T(8,128)}), f32[3,2,20,256,48]{4,3,2,1,0:T(8,128)}) %all-gather.5.cloned.1.call-update) | async-done | bytes 5898256 | tf_op jit(solution)/shard_map/all_gather | solution.py:93
  197.9 7.2 fusion
  205.2 7.1 fusion.1
  212.2 4.3 fusion.35
  216.6 3.8 fusion.33
  222.3 91.0 %all-gather.7.cloned.1.call-done = f32[2,20,3,2304]{1,0,2,3:T(2,128)} async-done(((f32[2,20,3,72]{1,0,2,3:T(2,128)}), f32[2,20,3,2304]{1,0,2,3:T(2,128)}) %all-gather.7.cloned.1.call-update) | async-done | bytes 1105936 | tf_op jit(solution)/shard_map/all_gather | solution.py:99
  313.3 10.0 %fusion.244 = (f32[1,20,3,2304]{1,0,2,3:T(1,128)}, f32[1,20,3,2304]{1,0,2,3:T(1,128)}) fusion(f32[2,20,3,2304]{1,0,2,3:T(2,128)} %all-gather.7.cloned.1.call-done), kind=kLoop, calls=%fused_computation.296 | loop fusion | bytes 2211840 | tf_op jit(solution)/shard_map/slice | solution.py:106
  323.3 11.2 %copy.429 = f32[1,20,3,2304]{3,2,1,0:T(4,128)} copy(f32[1,20,3,2304]{1,0,2,3:T(1,128)} %get-tuple-element.59) | data formatting | bytes 1105920 | tf_op jit(solution)/shard_map/squeeze | solution.py:105
  339.8 11.2 %copy.430 = f32[1,20,3,2304]{3,2,1,0:T(4,128)} copy(f32[1,20,3,2304]{1,0,2,3:T(1,128)} %get-tuple-element.58) | data formatting | bytes 1105920 | tf_op jit(solution)/shard_map/squeeze | solution.py:106
  360.5 5.6 reshape.225
  366.0 5.4 all-to-all-start.1
  371.6 2.8 fusion.18
  374.4 6.1 all-to-all-done.1
  382.4 5.4 reshape.226
  387.8 5.8 copy.314
  393.6 4.4 reshape.186
  399.4 10.1 %fusion.241 = (f32[20]{0:T(128)}, f32[20,8,16,256]{3,0,2,1:T(8,128)S(1)}, bf16[20,8,16,256]{3,0,2,1:T(8,128)(2,1)}) fusion(bf16[20,8,16,256]{3,2,1,0:T(8,128)(2,1)} %param.6, f32[256,48,1,1]{0,1,2,3:T(8,128)S(1)} %reshape.194, f32[20,8,16,48]{3,2,1,0:T(8,128)} %bitcast.337, f32[20,8,16,256]{3,0,2,1:T(8,128)} %fusion.18, f32[20]{0:T(128)S(1)} %copy-done.25), kind=kOutput, calls=%fused_computation.294 | convolution fusion | flops 393871360 | bytes 8405152 | tf_op jit(solution)/shard_map/km,zk->mz/dot_general | solution.py:114
  413.8 3.8 copy.319
  417.5 5.3 reshape.227
  422.8 12.3 %all_to_all.60 = f32[8,1,15360]{2,1,0:T(1,128)S(1)} all-to-all(f32[8,1,15360]{2,1,0:T(1,128)S(1)} %reshape.227), channel_id=1, replica_groups=mesh['gx'=32,'gy'=8] {'gy'}, dimensions={0} | all-to-all | bytes 983040 | tf_op jit(solution)/shard_map/all_to_all | solution.py:91
  437.0 5.3 reshape.228
  442.3 6.3 copy.320
  448.6 3.1 reshape.189
  454.3 137.9 %all-gather.9.cloned.1.call-done = f32[3,2,20,256,48]{4,3,2,1,0:T(8,128)} async-done(((f32[3,2,20,8,48]{4,3,2,1,0:T(8,128)}), f32[3,2,20,256,48]{4,3,2,1,0:T(8,128)}) %all-gather.9.cloned.1.call-update) | async-done | bytes 5898256 | tf_op jit(solution)/shard_map/all_gather | solution.py:93
  592.2 7.2 fusion.4
  599.4 7.1 fusion.5
  606.5 3.9 fusion.31
  610.4 4.1 fusion.29
  620.8 3.5 copy.447
  627.0 78.9 %all-reduce = (f32[20,20]{0,1:T(8,128)S(1)}, f32[20]{0:T(128)S(1)}) all-reduce(f32[20,20]{0,1:T(8,128)S(1)} %fusion.36, f32[20]{0:T(128)S(1)} %copy-done.24), channel_id=1, replica_groups=mesh['gx'=32,'gy'=8] {'gx','gy'}, use_global_device_ids=true, to_apply=%region_0.1 | all-reduce | flops 420 | bytes 3360 | tf_op jit(solution)/shard_map/psum | solution.py:158
  706.0 5.0 fusion.246
  711.0 10.0 %fusion.243 = (f32[1,20,3,2304]{1,0,2,3:T(1,128)}, f32[1,20,3,2304]{1,0,2,3:T(1,128)}) fusion(f32[2,20,3,2304]{1,0,2,3:T(2,128)} %all-gather.11.cloned.1.call-done), kind=kLoop, calls=%fused_computation.295 | loop fusion | bytes 2211840 | tf_op jit(solution)/shard_map/slice | solution.py:106
  721.0 9.8 %copy.433 = f32[1,20,3,2304]{3,2,1,0:T(4,128)S(1)} copy(f32[1,20,3,2304]{1,0,2,3:T(1,128)} %get-tuple-element.57) | data formatting | bytes 1105920 | tf_op jit(solution)/shard_map/squeeze | solution.py:105
  735.0 9.8 %copy.434 = f32[1,20,3,2304]{3,2,1,0:T(4,128)S(1)} copy(f32[1,20,3,2304]{1,0,2,3:T(1,128)} %get-tuple-element.56) | data formatting | bytes 1105920 | tf_op jit(solution)/shard_map/squeeze | solution.py:106
  753.3 5.7 reshape.229
  759.0 4.4 all-to-all-start.3
  766.8 2.9 copy.448
  776.0 5.3 reshape.230
  781.4 5.8 copy.337
  787.2 4.4 reshape.192
  792.0 5.0 add_convert_fusion
  (146 shorter events, 69.4 us)
Async XLA Ops:
  7.2 1.3 copy-start
  8.5 401.0 %copy-start.10 = (f32[256,48,1,1]{0,1,2,3:T(8,128)}, f32[256,48,1,1]{0,1,2,3:T(8,128)S(1)}, u32[]{:S(2)}) copy-start(f32[256,48,1,1]{0,1,2,3:T(8,128)S(1)} %reshape.194) | copy-start | bytes 147460
  19.7 15.8 %all-to-all-start = ((f32[8,1,15360]{2,1,0:T(1,128)}), f32[8,1,15360]{2,1,0:T(1,128)S(1)}, u32[]{:S(2)}, u32[]{:S(2)}) async-start(f32[8,1,15360]{2,1,0:T(1,128)} %reshape.223), calls=%async_computation | async-start | bytes 983040 | tf_op jit(solution)/shard_map/all_to_all | solution.py:91
  26.4 171.6 %all-gather.5.cloned.1.call-start = ((), (), s32[]{:S(2)}) async-start(), calls=%async_computation.4 | async-start | bytes 16220160 | tf_op jit(solution)/shard_map/all_gather | solution.py:93
  52.7 2.7 copy-start.9
  55.0 258.3 %all-gather.7.cloned.1.call-start = ((), (), s32[]{:S(2)}) async-start(), calls=%async_computation.5 | async-start | bytes 7299072 | tf_op jit(solution)/shard_map/all_gather | solution.py:99
  55.3 161.3 %copy-start.18 = (s32[3]{0:T(128)}, s32[3]{0:T(128)S(1)}, u32[]{:S(2)}) copy-start(s32[3]{0:T(128)S(1)} %compare_select_fusion) | copy-start | bytes 40
  55.3 165.9 %copy-start.22 = (f32[3]{0:T(128)}, f32[3]{0:T(128)S(1)}, u32[]{:S(2)}) copy-start(f32[3]{0:T(128)S(1)} %fusion.144) | copy-start | bytes 40
  56.2 164.7 %copy-start.5 = (bf16[1,20,20,3,72]{4,0,3,2,1:T(2,128)(2,1)}, bf16[1,20,20,3,72]{4,0,3,2,1:T(2,128)(2,1)S(1)}, u32[]{:S(2)}) copy-start(bf16[1,20,20,3,72]{4,0,3,2,1:T(2,128)(2,1)S(1)} %get-tuple-element.70) | copy-start | bytes 518404
  197.9 14.3 %copy-start.1 = (f32[3,2,20,256,48]{4,3,2,1,0:T(8,128)S(1)}, f32[3,2,20,256,48]{4,3,2,1,0:T(8,128)}, u32[]{:S(2)}) copy-start(f32[3,2,20,256,48]{4,3,2,1,0:T(8,128)} %all-gather.5.cloned.1.call-done) | copy-start | bytes 17694724
  220.8 102.5 %copy-start.12 = (f32[3,72,20]{1,0,2:T(4,128)}, f32[3,72,20]{1,0,2:T(4,128)S(1)}, u32[]{:S(2)}) copy-start(f32[3,72,20]{1,0,2:T(4,128)S(1)} %copy.440) | copy-start | bytes 51844
  220.8 102.5 %copy-start.14 = (f32[3,72,20]{1,0,2:T(4,128)}, f32[3,72,20]{1,0,2:T(4,128)S(1)}, u32[]{:S(2)}) copy-start(f32[3,72,20]{1,0,2:T(4,128)S(1)} %copy.439) | copy-start | bytes 51844
  222.2 132.6 %copy-start.16 = (s32[8]{0:T(128)}, s32[8]{0:T(128)S(1)}, u32[]{:S(2)}) copy-start(s32[8]{0:T(128)S(1)} %iota_add_fusion.1) | copy-start | bytes 100
  360.5 11.1 %copy-start.20 = (bf16[20,20]{1,0:T(8,128)(2,1)S(1)}, bf16[20,20]{1,0:T(8,128)(2,1)}, u32[]{:S(2)}) copy-start(bf16[20,20]{1,0:T(8,128)(2,1)} %param.8) | copy-start | bytes 2404
  366.0 14.5 %all-to-all-start.1 = ((f32[8,1,15360]{2,1,0:T(1,128)}), f32[8,1,15360]{2,1,0:T(1,128)S(1)}, u32[]{:S(2)}, u32[]{:S(2)}) async-start(f32[8,1,15360]{2,1,0:T(1,128)} %reshape.225), calls=%async_computation.1 | async-start | bytes 983040 | tf_op jit(solution)/shard_map/all_to_all | solution.py:112
  371.4 220.8 %all-gather.9.cloned.1.call-start = ((), (), s32[]{:S(2)}) async-start(), calls=%async_computation.6 | async-start | bytes 16220160 | tf_op jit(solution)/shard_map/all_gather | solution.py:93
  393.6 5.8 copy-start.25
  409.5 1.6 copy-start.3
  451.7 140.5 %copy-start.19 = (s32[3]{0:T(128)S(1)}, s32[3]{0:T(128)}, u32[]{:S(2)}) copy-start(s32[3]{0:T(128)} %copy-done.18) | copy-start | bytes 40
  454.0 257.0 %all-gather.11.cloned.1.call-start = ((), (), s32[]{:S(2)}) async-start(), calls=%async_computation.7 | async-start | bytes 7299072 | tf_op jit(solution)/shard_map/all_gather | solution.py:99
  592.2 14.3 %copy-start.2 = (f32[3,2,20,256,48]{4,3,2,1,0:T(8,128)S(1)}, f32[3,2,20,256,48]{4,3,2,1,0:T(8,128)}, u32[]{:S(2)}) copy-start(f32[3,2,20,256,48]{4,3,2,1,0:T(8,128)} %all-gather.9.cloned.1.call-done) | copy-start | bytes 17694724
  610.3 4.5 copy-start.23
  610.3 4.6 copy-start.6
  610.3 4.6 copy-start.13
  610.4 4.6 copy-start.15
  620.8 3.6 copy-start.4
  624.4 2.7 copy-start.24
  624.4 81.6 %copy-start.21 = (bf16[20,20]{1,0:T(8,128)(2,1)S(1)}, bf16[20,20]{1,0:T(8,128)(2,1)}, u32[]{:S(2)}) copy-start(bf16[20,20]{1,0:T(8,128)(2,1)} %param.8) | copy-start | bytes 2404
  721.0 10.9 %copy-start.17 = (s32[8]{0:T(128)S(1)}, s32[8]{0:T(128)}, u32[]{:S(2)}) copy-start(s32[8]{0:T(128)} %copy-done.16) | copy-start | bytes 100
  759.0 15.2 %all-to-all-start.3 = ((f32[8,1,15360]{2,1,0:T(1,128)}), f32[8,1,15360]{2,1,0:T(1,128)S(1)}, u32[]{:S(2)}, u32[]{:S(2)}) async-start(f32[8,1,15360]{2,1,0:T(1,128)} %reshape.229), calls=%async_computation.3 | async-start | bytes 983040 | tf_op jit(solution)/shard_map/all_to_all | solution.py:112
  769.7 2.3 copy-start.7
  769.8 2.3 copy-start.8
  787.2 4.8 copy-start.11
Sparse Core Ops, SparseCore 0:
  55.1 142.7 all-gather.4
  222.3 90.9 all-gather.6
  454.2 137.9 all-gather.8
  617.8 91.3 all-gather.10
where the time goes:
time: 811 us; the launch traced here: 804 us
  waiting for transfers between devices  386 us (48%)
  local copies, waits for them, and re-layouts  188 us (23%)
  matrix products  93.9 us (12%)
  blocking collectives  91.2 us (11%)
  starting transfers between devices  17.2 us (2%)
  between operations  14.7 us (2%)
  other arithmetic  12.6 us (2%)
    all_gather x2, waiting for transfers between devices, analyze(): portion = lax.all_gather(mode_data, 'gx', axis=3, tiled=True)  280 us
    all_gather x2, waiting for transfers between devices, synthesize(): portion = lax.all_gather(spectrum, 'gx', axis=3, tiled=True)  91 us
    psum x1, blocking collectives, local(): lax.psum((local_weight, local_bias), ('gx', 'gy'))  78.9 us
    unnamed x71, local copies, waits for them, and re-layouts  60.5 us
    squeeze x4, local copies, waits for them, and re-layouts, synthesize(): blocks[0]  24.1 us
    squeeze x4, local copies, waits for them, and re-layouts, synthesize(): blocks[1]  24.1 us
    slice x2, local copies, waits for them, and re-layouts, synthesize(): blocks[1]  20.1 us
  transfers between devices with their start and end apart: 7, of which 5 were waited for; matrix products, arithmetic and copies ran while one was open for 4% of the time, Pallas kernels for 0%

commit v1 on v0

--- a/solution.py
+++ b/solution.py
@@ -90,7 +90,9 @@
         )
         columns = lax.all_to_all(spectra, "gy", split_axis=0, concat_axis=3, tiled=True)
         mode_data = forward_y(columns.reshape(blocks_z, 2, channels, rows_x, full_y), phases_full_y)
-        portion = lax.all_gather(mode_data, "gx", axis=3, tiled=True)
+        portion = jnp.concatenate(
+            lax.all_to_all(jnp.stack([mode_data] * lax.axis_size("gx")), "gx", 0, 0), axis=3
+        )
         places = jnp.arange(portion.shape[3], dtype=jnp.int32)
         owned = kx_terms(portion, places, own_first, pair_rows)
         return jnp.transpose(owned.reshape(pair_rows, blocks_z, 2, channels), (2, 3, 1, 0))

time: 811 us -> 1020 us (1.26)
  waiting for transfers between devices: 386 us -> 239 us
  blocking collectives: 91.2 us -> 226 us
  other arithmetic: 12.6 us -> 119 us
  local copies, waits for them, and re-layouts: 188 us -> 292 us
  starting transfers between devices: 17.2 us -> 27.7 us
    all_gather x2 -> x0, waiting for transfers between devices: 280 us -> none  [analyze(): portion = lax.all_gather(mode_data, 'gx', axis=3, tiled=True)]
    all_to_all x0 -> x1, blocking collectives: none -> 136 us  [analyze(): lax.all_to_all(jnp.stack([mode_data] * lax.axis_size('gx')), 'gx', 0, 0)]
    all_to_all x0 -> x1, waiting for transfers between devices: none -> 128 us  [analyze(): lax.all_to_all(jnp.stack([mode_data] * lax.axis_size('gx')), 'gx', 0, 0)]
    all_to_all x0 -> x2, other arithmetic: none -> 108 us  [analyze(): lax.all_to_all(jnp.stack([mode_data] * lax.axis_size('gx')), 'gx', 0, 0)]
    unnamed x71 -> x75, local copies, waits for them, and re-layouts: 60.5 us -> 123 us
    reshape x0 -> x2, local copies, waits for them, and re-layouts: none -> 26.4 us  [analyze(): jnp.concatenate(lax.all_to_all(jnp.stack([mode_data] * lax.axis_size('gx'...]
    another operation x0 -> x2, local copies, waits for them, and re-layouts: none -> 14.9 us  [analyze(): jnp.stack([mode_data] * lax.axis_size('gx'))]
    all_to_all x0 -> x1, starting transfers between devices: none -> 10.6 us  [analyze(): lax.all_to_all(jnp.stack([mode_data] * lax.axis_size('gx')), 'gx', 0, 0)]
  transfers between devices with their start and end apart: 7 -> 6, of which waited for: 5 -> 4; matrix products, arithmetic and copies ran while one was open for 4% -> 3% of each run, Pallas kernels for 0% -> 0%
where the time goes in v1:
time: 1020 us; the launch traced here: 1010 us
  local copies, waits for them, and re-layouts  292 us (29%)
  waiting for transfers between devices  239 us (23%)
  blocking collectives  226 us (22%)
  other arithmetic  119 us (12%)
  matrix products  93.8 us (9%)
  starting transfers between devices  27.7 us (3%)
  between operations  15 us (1%)
    all_to_all x1, blocking collectives, analyze(): lax.all_to_all(jnp.stack([mode_data] * lax.axis_size('gx')), 'gx', 0, 0)  136 us
    all_to_all x1, waiting for transfers between devices, analyze(): lax.all_to_all(jnp.stack([mode_data] * lax.axis_size('gx')), 'gx', 0, 0)  128 us
    unnamed x75, local copies, waits for them, and re-layouts  123 us
    all_to_all x2, other arithmetic, analyze(): lax.all_to_all(jnp.stack([mode_data] * lax.axis_size('gx')), 'gx', 0, 0)  108 us
    all_gather x2, waiting for transfers between devices, synthesize(): portion = lax.all_gather(spectrum, 'gx', axis=3, tiled=True)  95.4 us
    psum x1, blocking collectives, local(): lax.psum((local_weight, local_bias), ('gx', 'gy'))  77.1 us
    reshape x2, local copies, waits for them, and re-layouts, analyze(): jnp.concatenate(lax.all_to_all(jnp.stack([mode_data] * lax.axis_size('gx'...  26.4 us
    squeeze x4, local copies, waits for them, and re-layouts, synthesize(): blocks[1]  24.3 us
  transfers between devices with their start and end apart: 6, of which 4 were waited for; matrix products, arithmetic and copies ran while one was open for 3% of the time, Pallas kernels for 0%

profile of v1, /device:TPU:1, one launch (start us, length us, event | category | flops | bytes accessed | tf_op | source)
XLA Modules:
  0.0 1012.6 jit_solution(10077876600174489311)
XLA Ops:
  14.2 5.5 reshape.243
  19.7 7.1 all-to-all-start
  26.9 9.1 all-to-all-done
  38.3 5.3 reshape.244
  43.6 6.3 copy.277
  54.5 7.5 stack.58
  62.0 20.2 %reshape.245 = f32[32,1,46080]{2,1,0:T(1,128)} reshape(f32[32,3,2,20,8,48]{5,4,3,2,1,0:T(8,128)} %stack.58) | data formatting | bytes 11796480
  82.2 10.6 %all-to-all-start.1 = ((f32[32,1,46080]{2,1,0:T(1,128)}), f32[32,1,46080]{2,1,0:T(1,128)}, u32[]{:S(2)}, u32[]{:S(2)}) async-start(f32[32,1,46080]{2,1,0:T(1,128)} %reshape.245), calls=%async_computation.1 | async-start | bytes 11796480 | tf_op jit(solution)/shard_map/all_to_all | solution.py:94
  94.0 127.7 %all-to-all-done.1 = f32[32,1,46080]{2,1,0:T(1,128)} async-done(((f32[32,1,46080]{2,1,0:T(1,128)}), f32[32,1,46080]{2,1,0:T(1,128)}, u32[]{:S(2)}, u32[]{:S(2)}) %all-to-all-start.1) | async-done | bytes 5898272 | tf_op jit(solution)/shard_map/all_to_all | solution.py:94
  221.7 54.2 %reduce.18 = f32[32,46080]{1,0:T(8,128)} reduce(f32[32,1,46080]{2,1,0:T(1,128)} %all-to-all-done.1, f32[]{:T(128)} %broadcast.402), dimensions={1}, to_apply=%all_to_all.53.reduce_sub_computation | reduce | bytes 11796484 | tf_op jit(solution)/shard_map/all_to_all | solution.py:94
  275.9 11.2 %reshape.246 = f32[32,3,2,20,8,48]{5,4,3,2,1,0:T(8,128)} reshape(f32[32,46080]{1,0:T(8,128)} %reduce.18) | data formatting | bytes 11796480
  287.1 13.2 %copy_bitcast_fusion.1 = f32[3,2,20,256,48]{4,3,2,1,0:T(8,128)} fusion(f32[32,3,2,20,8,48]{5,4,3,2,1,0:T(8,128)} %reshape.246), kind=kLoop, calls=%fused_computation.1 | loop fusion | bytes 11796480 | tf_op jit(solution)/shard_map/reshape | solution.py:93
  300.3 7.2 fusion
  307.5 7.1 fusion.1
  324.5 95.4 %all-gather.3.cloned.1.call-done = f32[2,20,3,2304]{1,0,2,3:T(2,128)} async-done(((f32[2,20,3,72]{1,0,2,3:T(2,128)}), f32[2,20,3,2304]{1,0,2,3:T(2,128)}) %all-gather.3.cloned.1.call-update) | async-done | bytes 1105936 | tf_op jit(solution)/shard_map/all_gather | solution.py:101
  420.0 10.0 fusion.244
  430.0 11.2 %copy.401 = f32[1,20,3,2304]{3,2,1,0:T(4,128)} copy(f32[1,20,3,2304]{1,0,2,3:T(1,128)} %get-tuple-element.59) | data formatting | bytes 1105920 | tf_op jit(solution)/shard_map/squeeze | solution.py:107
  446.4 11.2 %copy.402 = f32[1,20,3,2304]{3,2,1,0:T(4,128)} copy(f32[1,20,3,2304]{1,0,2,3:T(1,128)} %get-tuple-element.58) | data formatting | bytes 1105920 | tf_op jit(solution)/shard_map/squeeze | solution.py:108
  467.3 5.6 reshape.247
  472.8 5.4 all-to-all-start.2
  481.0 6.3 all-to-all-done.2
  489.1 5.4 reshape.248
  494.5 6.2 copy.295
  500.7 4.4 reshape.204
  506.5 10.1 fusion.241
  524.6 5.0 reshape.249
  529.6 12.3 %all_to_all.70 = f32[8,1,15360]{2,1,0:T(1,128)S(1)} all-to-all(f32[8,1,15360]{2,1,0:T(1,128)S(1)} %reshape.249), channel_id=1, replica_groups=mesh['gx'=32,'gy'=8] {'gy'}, dimensions={0} | all-to-all | bytes 983040 | tf_op jit(solution)/shard_map/all_to_all | solution.py:91
  543.7 5.3 reshape.250
  549.1 6.3 copy.301
  560.0 7.5 stack.70
  567.4 20.2 %reshape.251 = f32[32,1,46080]{2,1,0:T(1,128)} reshape(f32[32,3,2,20,8,48]{5,4,3,2,1,0:T(8,128)} %stack.70) | data formatting | bytes 11796480
  587.6 136.5 %all_to_all.71 = f32[32,1,46080]{2,1,0:T(1,128)} all-to-all(f32[32,1,46080]{2,1,0:T(1,128)} %reshape.251), channel_id=1, replica_groups=mesh['gx'=32,'gy'=8] {'gx'}, dimensions={0} | all-to-all | bytes 11796480 | tf_op jit(solution)/shard_map/all_to_all | solution.py:94
  724.1 54.2 %reduce.21 = f32[32,46080]{1,0:T(8,128)} reduce(f32[32,1,46080]{2,1,0:T(1,128)} %all_to_all.71, f32[]{:T(128)} %broadcast.402), dimensions={1}, to_apply=%all_to_all.60.reduce_sub_computation | reduce | bytes 11796484 | tf_op jit(solution)/shard_map/all_to_all | solution.py:94
  778.3 11.4 %reshape.252 = f32[32,3,2,20,8,48]{5,4,3,2,1,0:T(8,128)} reshape(f32[32,46080]{1,0:T(8,128)} %reduce.21) | data formatting | bytes 11796480
  789.7 13.2 %copy_bitcast_fusion = f32[3,2,20,256,48]{4,3,2,1,0:T(8,128)} fusion(f32[32,3,2,20,8,48]{5,4,3,2,1,0:T(8,128)} %reshape.252), kind=kLoop, calls=%fused_computation | loop fusion | bytes 11796480 | tf_op jit(solution)/shard_map/reshape | solution.py:93
  802.9 7.2 fusion.4
  810.1 7.1 fusion.5
  837.7 77.1 %all-reduce = (f32[20,20]{0,1:T(8,128)S(1)}, f32[20]{0:T(128)S(1)}) all-reduce(f32[20,20]{0,1:T(8,128)S(1)} %fusion.36, f32[20]{0:T(128)S(1)} %copy-done.24), channel_id=1, replica_groups=mesh['gx'=32,'gy'=8] {'gx','gy'}, use_global_device_ids=true, to_apply=%region_0.1 | all-reduce | flops 420 | bytes 3360 | tf_op jit(solution)/shard_map/psum | solution.py:160
  914.8 5.0 fusion.246
  919.8 10.0 fusion.243
  929.8 9.8 copy.405
  943.8 9.8 copy.406
  962.0 5.7 reshape.253
  967.7 4.4 all-to-all-start.5
  984.7 5.3 reshape.254
  990.0 5.8 copy.317
  995.8 4.4 reshape.212
  1000.6 5.0 add_convert_fusion
  (153 shorter events, 106.0 us)
Async XLA Ops:
  7.2 1.3 copy-start
  8.5 508.1 %copy-start.10 = (f32[256,48,1,1]{0,1,2,3:T(8,128)}, f32[256,48,1,1]{0,1,2,3:T(8,128)S(1)}, u32[]{:S(2)}) copy-start(f32[256,48,1,1]{0,1,2,3:T(8,128)S(1)} %reshape.214) | copy-start | bytes 147460
  19.7 16.2 %all-to-all-start = ((f32[8,1,15360]{2,1,0:T(1,128)}), f32[8,1,15360]{2,1,0:T(1,128)S(1)}, u32[]{:S(2)}, u32[]{:S(2)}) async-start(f32[8,1,15360]{2,1,0:T(1,128)} %reshape.243), calls=%async_computation | async-start | bytes 983040 | tf_op jit(solution)/shard_map/all_to_all | solution.py:91
  82.2 10.9 %copy-start.9 = (bf16[2,20,20,3,72]{4,0,3,2,1:T(2,128)(2,1)S(1)}, bf16[2,20,20,3,72]{4,0,3,2,1:T(2,128)(2,1)}, u32[]{:S(2)}) copy-start(bf16[2,20,20,3,72]{4,0,3,2,1:T(2,128)(2,1)} %param.7) | copy-start | bytes 1036804
  82.2 139.5 %all-to-all-start.1 = ((f32[32,1,46080]{2,1,0:T(1,128)}), f32[32,1,46080]{2,1,0:T(1,128)}, u32[]{:S(2)}, u32[]{:S(2)}) async-start(f32[32,1,46080]{2,1,0:T(1,128)} %reshape.245), calls=%async_computation.1 | async-start | bytes 11796480 | tf_op jit(solution)/shard_map/all_to_all | solution.py:94
  92.8 327.2 %all-gather.3.cloned.1.call-start = ((), (), s32[]{:S(2)}) async-start(), calls=%async_computation.6 | async-start | bytes 7299072 | tf_op jit(solution)/shard_map/all_gather | solution.py:101
  93.0 225.8 %copy-start.18 = (s32[3]{0:T(128)}, s32[3]{0:T(128)S(1)}, u32[]{:S(2)}) copy-start(s32[3]{0:T(128)S(1)} %compare_select_fusion) | copy-start | bytes 40
  93.1 230.5 %copy-start.22 = (f32[3]{0:T(128)}, f32[3]{0:T(128)S(1)}, u32[]{:S(2)}) copy-start(f32[3]{0:T(128)S(1)} %fusion.144) | copy-start | bytes 40
  94.0 229.2 %copy-start.5 = (bf16[1,20,20,3,72]{4,0,3,2,1:T(2,128)(2,1)}, bf16[1,20,20,3,72]{4,0,3,2,1:T(2,128)(2,1)S(1)}, u32[]{:S(2)}) copy-start(bf16[1,20,20,3,72]{4,0,3,2,1:T(2,128)(2,1)S(1)} %get-tuple-element.70) | copy-start | bytes 518404
  300.3 14.3 %copy-start.2 = (f32[3,2,20,256,48]{4,3,2,1,0:T(8,128)S(1)}, f32[3,2,20,256,48]{4,3,2,1,0:T(8,128)}, u32[]{:S(2)}) copy-start(f32[3,2,20,256,48]{4,3,2,1,0:T(8,128)} %copy_bitcast_fusion.1) | copy-start | bytes 17694724
  323.1 106.9 %copy-start.12 = (f32[3,72,20]{1,0,2:T(4,128)}, f32[3,72,20]{1,0,2:T(4,128)S(1)}, u32[]{:S(2)}) copy-start(f32[3,72,20]{1,0,2:T(4,128)S(1)} %copy.416) | copy-start | bytes 51844
  323.1 106.8 %copy-start.14 = (f32[3,72,20]{1,0,2:T(4,128)}, f32[3,72,20]{1,0,2:T(4,128)S(1)}, u32[]{:S(2)}) copy-start(f32[3,72,20]{1,0,2:T(4,128)S(1)} %copy.415) | copy-start | bytes 51844
  324.5 137.1 %copy-start.16 = (s32[8]{0:T(128)}, s32[8]{0:T(128)S(1)}, u32[]{:S(2)}) copy-start(s32[8]{0:T(128)S(1)} %iota_add_fusion.1) | copy-start | bytes 100
  467.3 10.9 %copy-start.20 = (bf16[20,20]{1,0:T(8,128)(2,1)S(1)}, bf16[20,20]{1,0:T(8,128)(2,1)}, u32[]{:S(2)}) copy-start(bf16[20,20]{1,0:T(8,128)(2,1)} %param.8) | copy-start | bytes 2404
  472.8 14.5 %all-to-all-start.2 = ((f32[8,1,15360]{2,1,0:T(1,128)}), f32[8,1,15360]{2,1,0:T(1,128)S(1)}, u32[]{:S(2)}, u32[]{:S(2)}) async-start(f32[8,1,15360]{2,1,0:T(1,128)} %reshape.247), calls=%async_computation.2 | async-start | bytes 983040 | tf_op jit(solution)/shard_map/all_to_all | solution.py:114
  478.2 441.6 %all-gather.5.cloned.1.call-start = ((), (), s32[]{:S(2)}) async-start(), calls=%async_computation.7 | async-start | bytes 7299072 | tf_op jit(solution)/shard_map/all_gather | solution.py:101
  500.7 5.8 copy-start.25
  516.6 1.6 copy-start.3
  789.7 13.2 %copy-start.19 = (s32[3]{0:T(128)S(1)}, s32[3]{0:T(128)}, u32[]{:S(2)}) copy-start(s32[3]{0:T(128)} %copy-done.18) | copy-start | bytes 40
  802.9 14.3 %copy-start.1 = (f32[3,2,20,256,48]{4,3,2,1,0:T(8,128)S(1)}, f32[3,2,20,256,48]{4,3,2,1,0:T(8,128)}, u32[]{:S(2)}) copy-start(f32[3,2,20,256,48]{4,3,2,1,0:T(8,128)} %copy_bitcast_fusion) | copy-start | bytes 17694724
  821.2 4.3 copy-start.23
  821.2 4.3 copy-start.6
  821.2 4.4 copy-start.13
  821.2 4.4 copy-start.15
  831.5 3.5 copy-start.4
  835.0 2.7 copy-start.24
  835.0 79.8 %copy-start.21 = (bf16[20,20]{1,0:T(8,128)(2,1)S(1)}, bf16[20,20]{1,0:T(8,128)(2,1)}, u32[]{:S(2)}) copy-start(bf16[20,20]{1,0:T(8,128)(2,1)} %param.8) | copy-start | bytes 2404
  929.8 10.9 %copy-start.17 = (s32[8]{0:T(128)S(1)}, s32[8]{0:T(128)}, u32[]{:S(2)}) copy-start(s32[8]{0:T(128)} %copy-done.16) | copy-start | bytes 100
  967.7 15.2 %all-to-all-start.5 = ((f32[8,1,15360]{2,1,0:T(1,128)}), f32[8,1,15360]{2,1,0:T(1,128)S(1)}, u32[]{:S(2)}, u32[]{:S(2)}) async-start(f32[8,1,15360]{2,1,0:T(1,128)} %reshape.253), calls=%async_computation.5 | async-start | bytes 983040 | tf_op jit(solution)/shard_map/all_to_all | solution.py:114
  978.4 2.4 copy-start.7
  978.4 2.3 copy-start.8
  995.8 4.8 copy-start.11
Sparse Core Ops, SparseCore 0:
  324.6 95.3 all-gather.2
  828.5 88.4 all-gather.4
